TPU v7x, 32 devices: a whole 2x2x4 slice. The times are simulated.
32 devices in a mesh: dp: 8 (over z, x), tensor: 4 (over y, core).
Axes of the slice: x: 2, y: 2, z: 4, core: 2. Of those that a mesh axis runs over, the one named last changes fastest.
Arguments:
- tokens: bfloat16 [24, 512, 768], P('dp', None, 'tensor'), may hold values from -6 to 6
- cotangent: bfloat16 [24, 512, 768], P('dp', None, 'tensor'), may hold values from -6 to 6
- prev_logits: bfloat16 [24, 12, 512, 512], P('dp', 'tensor'), may hold values from -6 to 6
- segment_ids: int32 [24, 512], P('dp'), may hold values from 0 to 5, never falling along the last dimension, each value on 1 to 256 neighbouring positions
- w_qkv: float32 [768, 3, 768], P('dp', None, 'tensor'), may hold values from -0.21875 to 0.21875
- b_qv: float32 [2, 768], P(None, 'tensor'), may hold values from -3 to 3
- w_out: float32 [768, 768], P('tensor', 'dp'), may hold values from -0.625 to 0.625
- w_up: float32 [768, 3072], P('dp', 'tensor'), may hold values from -0.21875 to 0.21875
- b_up: float32 [3072], P('tensor'), may hold values from -3 to 3
- w_down: float32 [3072, 768], P('tensor', 'dp'), may hold values from -0.109375 to 0.109375
- biases: float32 [2, 768], replicated, may hold values from -3 to 3
- gains: float32 [2, 768], replicated, may hold values from 0.25 to 1.75
- shifts: float32 [2, 768], replicated, may hold values from -3 to 3
Outputs:
- activations: bfloat16 [24, 512, 768], P('dp', None, 'tensor')
- raw_logits: bfloat16 [24, 12, 512, 512], P('dp', 'tensor')
- input_grad: bfloat16 [24, 512, 768], P('dp', None, 'tensor')
- logits_grad: bfloat16 [24, 12, 512, 512], P('dp', 'tensor')
- grad_qkv: float32 [768, 3, 768], P(None, None, 'tensor')
- grad_b_qv: float32 [2, 768], P(None, 'tensor')
- grad_out: float32 [768, 768], P('tensor')
- grad_up: float32 [768, 3072], P(None, 'tensor')
- grad_b_up: float32 [3072], P('tensor')
- grad_down: float32 [3072, 768], P('tensor')
- grad_biases: float32 [2, 768], replicated
- grad_gains: float32 [2, 768], replicated
- grad_shifts: float32 [2, 768], replicated
Inputs may be any that keep to these rules, and one draw needn't show every extreme that they name: `segment_ids`: in each row the segment number never falls; each segment has 1 to 256 slots and one has exactly that many; a query attends only to keys of its own segment.
All inputs are finite; a program needn't handle non-finite values.
Results may differ from a plain program's by a relative error of at most 0.02.
Values may be sent and summed in bfloat16 or wider, within the bound.
No kernel may reach another device: no remote copies, remote signals or barrier semaphores. Data moves between devices by JAX's collectives and lax.ppermute only.
A program may use at most 192 MiB of HBM per device.

v0:
```python
import math
import jax
import jax.numpy as jnp
from jax import lax
from jax.sharding import PartitionSpec as P

EPS = 1e-06
NEG = -1e30


def gelu_exact(values):
    return jax.nn.gelu(values, approximate=False)


def norm_forward(summed, gain_row, shift_row):
    row_mean = jnp.mean(summed, axis=-1, keepdims=True)
    centered = summed - row_mean
    inv_std = lax.rsqrt(jnp.mean(centered * centered, axis=-1, keepdims=True) + EPS)
    normed = centered * inv_std
    return (normed * gain_row + shift_row, normed, inv_std)


def norm_backward(grad_output, normed, inv_std, gain_row):
    scaled = grad_output * gain_row
    inner = (
        scaled
        - jnp.mean(scaled, axis=-1, keepdims=True)
        - normed * jnp.mean(scaled * normed, axis=-1, keepdims=True)
    )
    return inner * inv_std


def branch_total(partial_value):
    return lax.psum(partial_value.astype(jnp.bfloat16), "tensor").astype(jnp.float32)


def attend_rows(query, keys, values, previous, segment, inv_root):
    allowed = (segment[:, None] == segment[None, :])[None]
    scores = jnp.einsum(
        "qhe,khe->hqk", query, keys, preferred_element_type=jnp.float32
    ) * inv_root + previous.astype(jnp.float32)
    masked = jnp.where(allowed, scores, NEG)
    row_max = jnp.max(masked, axis=-1, keepdims=True)
    expanded = jnp.exp(masked - row_max)
    row_sum = jnp.sum(expanded, axis=-1, keepdims=True)
    probability = (expanded / row_sum).astype(jnp.bfloat16)
    output = jnp.einsum(
        "hqk,khe->qhe", probability, values, preferred_element_type=jnp.float32
    ).astype(jnp.bfloat16)
    log_total = row_max[..., 0] + jnp.log(row_sum[..., 0])
    return (output, scores.astype(jnp.bfloat16), log_total)


def attend_back(query, keys, values, previous, segment, log_total, grad_heads, inv_root):
    allowed = (segment[:, None] == segment[None, :])[None]
    scores = jnp.einsum(
        "qhe,khe->hqk", query, keys, preferred_element_type=jnp.float32
    ) * inv_root + previous.astype(jnp.float32)
    probability = jnp.where(allowed, jnp.exp(scores - log_total[..., None]), 0.0)
    grad_prob = jnp.einsum("qhe,khe->hqk", grad_heads, values, preferred_element_type=jnp.float32)
    grad_values = jnp.einsum(
        "hqk,qhe->khe",
        probability.astype(jnp.bfloat16),
        grad_heads,
        preferred_element_type=jnp.float32,
    )
    inner = jnp.sum(grad_prob * probability, axis=-1, keepdims=True)
    grad_scores = (probability * (grad_prob - inner)).astype(jnp.bfloat16)
    grad_query = (
        jnp.einsum("hqk,khe->qhe", grad_scores, keys, preferred_element_type=jnp.float32) * inv_root
    )
    grad_keys = (
        jnp.einsum("hqk,qhe->khe", grad_scores, query, preferred_element_type=jnp.float32)
        * inv_root
    )
    return (grad_query, grad_keys, grad_values, grad_scores)


def body(
    tokens,
    cotangent,
    prev_logits,
    segment_ids,
    w_qkv,
    b_qv,
    w_out,
    w_up,
    b_up,
    w_down,
    biases,
    gains,
    shifts,
):
    row_count, slot_count, part_width = tokens.shape
    full_width = part_width * lax.axis_size("tensor")
    local_width = b_qv.shape[1]
    heads_here = prev_logits.shape[1]
    head_size = local_width // heads_here
    token_count = row_count * slot_count
    inv_root = 1.0 / math.sqrt(head_size)
    my_cols = lax.axis_index("tensor") * part_width
    gathered_x, gathered_dy = (
        lax.all_gather(tokens, "tensor", axis=2, tiled=True),
        lax.all_gather(cotangent, "tensor", axis=2, tiled=True),
    )
    inputs_bf = gathered_x.reshape(token_count, full_width)
    grad_final = gathered_dy.reshape(token_count, full_width).astype(jnp.float32)
    qkv_weight, up_weight = (
        lax.all_gather(w_qkv.astype(jnp.bfloat16), "dp", axis=0, tiled=True),
        lax.all_gather(w_up.astype(jnp.bfloat16), "dp", axis=0, tiled=True),
    )
    out_weight, down_weight = (
        lax.all_gather(w_out.astype(jnp.bfloat16), "dp", axis=1, tiled=True),
        lax.all_gather(w_down.astype(jnp.bfloat16), "dp", axis=1, tiled=True),
    )
    qkv_matrix = qkv_weight.reshape(full_width, 3 * local_width)
    qkv_bias = jnp.stack([b_qv[0], jnp.zeros_like(b_qv[0]), b_qv[1]])

    def project(source, matrix):
        product = jnp.dot(source, matrix, preferred_element_type=jnp.float32).reshape(
            token_count, 3, local_width
        )
        return (
            (product + qkv_bias)
            .astype(jnp.bfloat16)
            .reshape(row_count, slot_count, 3, heads_here, head_size)
        )

    def attend_all(packed):

        def one_row(row_items):
            return attend_rows(
                row_items[0], row_items[1], row_items[2], row_items[3], row_items[4], inv_root
            )

        return lax.map(
            one_row, (packed[:, :, 0], packed[:, :, 1], packed[:, :, 2], prev_logits, segment_ids)
        )

    qkv_all = project(inputs_bf, qkv_matrix)
    attn_heads, raw_scores, log_total = attend_all(qkv_all)
    attn_flat = attn_heads.reshape(token_count, local_width)
    attn_partial = jnp.dot(attn_flat, out_weight, preferred_element_type=jnp.float32)
    first_out, normed_one, inv_one = norm_forward(
        inputs_bf.astype(jnp.float32) + branch_total(attn_partial) + biases[0], gains[0], shifts[0]
    )
    first_bf = first_out.astype(jnp.bfloat16)
    hidden = jnp.dot(first_bf, up_weight, preferred_element_type=jnp.float32) + b_up
    activated = gelu_exact(hidden).astype(jnp.bfloat16)
    ffn_partial = jnp.dot(activated, down_weight, preferred_element_type=jnp.float32)
    final_out, normed_two, inv_two = norm_forward(
        first_out + branch_total(ffn_partial) + biases[1], gains[1], shifts[1]
    )
    block_out = (
        lax.dynamic_slice_in_dim(final_out, my_cols, part_width, 1)
        .reshape(row_count, slot_count, part_width)
        .astype(jnp.bfloat16)
    )
    grad_gain_two = jnp.sum(grad_final * normed_two, axis=0)
    grad_shift_two = jnp.sum(grad_final, axis=0)
    grad_sum_two = norm_backward(grad_final, normed_two, inv_two, gains[1])
    grad_bias_down = jnp.sum(grad_sum_two, axis=0)
    grad_sum_two_bf = grad_sum_two.astype(jnp.bfloat16)
    again = lax.optimization_barrier((inputs_bf, qkv_matrix, first_bf, up_weight, grad_sum_two_bf))
    qkv_back = project(again[0], again[1])
    attn_back = attend_all(qkv_back)[0].reshape(token_count, local_width)
    first_back = again[2]
    hidden_back = jnp.dot(first_back, again[3], preferred_element_type=jnp.float32) + b_up
    act_back = gelu_exact(hidden_back).astype(jnp.bfloat16)
    grad_down = jnp.dot(act_back.T, grad_sum_two_bf, preferred_element_type=jnp.float32)
    grad_act = jnp.dot(grad_sum_two_bf, down_weight.T, preferred_element_type=jnp.float32)
    grad_hidden = jax.vjp(gelu_exact, hidden_back)[1](grad_act)[0]
    grad_bias_up = jnp.sum(grad_hidden, axis=0)
    grad_hidden_bf = grad_hidden.astype(jnp.bfloat16)
    grad_up = jnp.dot(first_back.T, grad_hidden_bf, preferred_element_type=jnp.float32)
    ffn_summed = (grad_up, grad_bias_up, grad_down, grad_bias_down, grad_gain_two, grad_shift_two)
    first_partial = jnp.dot(grad_hidden_bf, up_weight.T, preferred_element_type=jnp.float32)
    grad_first = grad_sum_two + branch_total(first_partial)
    grad_gain_one = jnp.sum(grad_first * normed_one, axis=0)
    grad_shift_one = jnp.sum(grad_first, axis=0)
    grad_sum_one = norm_backward(grad_first, normed_one, inv_one, gains[0])
    grad_bias_out = jnp.sum(grad_sum_one, axis=0)
    grad_sum_one_bf = grad_sum_one.astype(jnp.bfloat16)
    own_grad = lax.dynamic_slice_in_dim(grad_sum_one, my_cols, part_width, 1)
    grad_out = jnp.dot(attn_back.T, grad_sum_one_bf, preferred_element_type=jnp.float32)
    grad_heads = jnp.dot(grad_sum_one_bf, out_weight.T, preferred_element_type=jnp.float32).astype(
        jnp.bfloat16
    )
    grad_heads = grad_heads.reshape(row_count, slot_count, heads_here, head_size)

    def back_row(row_items):
        return attend_back(
            row_items[0],
            row_items[1],
            row_items[2],
            row_items[3],
            row_items[4],
            row_items[5],
            row_items[6],
            inv_root,
        )

    grad_query, grad_keys, grad_values, grad_scores = lax.map(
        back_row,
        (
            qkv_back[:, :, 0],
            qkv_back[:, :, 1],
            qkv_back[:, :, 2],
            prev_logits,
            segment_ids,
            log_total,
            grad_heads,
        ),
    )
    grad_qkv_full = jnp.stack([grad_query, grad_keys, grad_values], axis=2).reshape(
        token_count, 3, local_width
    )
    grad_b_qv = jnp.stack(
        [jnp.sum(grad_qkv_full[:, 0], axis=0), jnp.sum(grad_qkv_full[:, 2], axis=0)]
    )
    grad_qkv_bf = grad_qkv_full.reshape(token_count, 3 * local_width).astype(jnp.bfloat16)
    grad_qkv = jnp.dot(inputs_bf.T, grad_qkv_bf, preferred_element_type=jnp.float32).reshape(
        full_width, 3, local_width
    )
    grad_input_part = jnp.dot(grad_qkv_bf, qkv_matrix.T, preferred_element_type=jnp.float32)
    grad_input = (
        lax.psum_scatter(
            grad_input_part.astype(jnp.bfloat16), "tensor", scatter_dimension=1, tiled=True
        ).astype(jnp.float32)
        + own_grad
    )
    grad_input = grad_input.reshape(row_count, slot_count, part_width).astype(jnp.bfloat16)
    every_sum = lax.psum(
        (
            grad_qkv,
            grad_b_qv,
            grad_out,
            grad_bias_out,
            grad_gain_one,
            grad_shift_one,
            ffn_summed[0],
            ffn_summed[1],
            ffn_summed[2],
            ffn_summed[3],
            ffn_summed[4],
            ffn_summed[5],
        ),
        "dp",
    )
    attn_summed = every_sum[:6]
    ffn_final = every_sum[6:]
    grad_biases_all = jnp.stack([attn_summed[3], ffn_final[3]])
    grad_gains_all = jnp.stack([attn_summed[4], ffn_final[4]])
    grad_shifts_all = jnp.stack([attn_summed[5], ffn_final[5]])
    return (
        block_out,
        raw_scores,
        grad_input,
        grad_scores,
        attn_summed[0],
        attn_summed[1],
        attn_summed[2],
        ffn_final[0],
        ffn_final[1],
        ffn_final[2],
        grad_biases_all,
        grad_gains_all,
        grad_shifts_all,
    )


def solution(mesh):
    placed = (
        P("dp", None, "tensor"),
        P("dp", None, "tensor"),
        P("dp", "tensor", None, None),
        P("dp", None),
        P("dp", None, "tensor"),
        P(None, "tensor"),
        P("tensor", "dp"),
        P("dp", "tensor"),
        P("tensor"),
        P("tensor", "dp"),
        P(),
        P(),
        P(),
    )
    return jax.shard_map(
        body,
        mesh=mesh,
        in_specs=placed,
        out_specs=(
            P("dp", None, "tensor"),
            P("dp", "tensor", None, None),
            P("dp", None, "tensor"),
            P("dp", "tensor", None, None),
            P(None, None, "tensor"),
            P(None, "tensor"),
            P("tensor", None),
            P(None, "tensor"),
            P("tensor"),
            P("tensor", None),
            P(),
            P(),
            P(),
        ),
        check_vma=False,
    )
```

profile of v0, /device:TPU:0, one launch (start us, length us, event | category | flops | bytes accessed | tf_op | source)
XLA Modules:
  0.0 772.9 jit_solution(10725266084257419247)
XLA Ops:
  10.9 38.8 %all_gather.19 = bf16[768,3,192]{2,1,0:T(4,128)(2,1)S(1)} all-gather(bf16[96,3,192]{2,1,0:T(4,128)(2,1)S(1)} %copy.112), channel_id=1, replica_groups=mesh['dp'=8,'tensor'=4] {'dp'}, dimensions={0}, use_global_device_ids=true | all-gather | bytes 995328 | tf_op jit(solution)/shard_map/all_gather | solution.py:109
  50.7 7.0 copy.117
  57.7 33.0 %all_gather.20 = bf16[192,768]{0,1:T(8,128)(2,1)} all-gather(bf16[192,96]{0,1:T(8,128)(2,1)S(1)} %copy.119), channel_id=1, replica_groups=mesh['dp'=8,'tensor'=4] {'dp'}, dimensions={1}, use_global_device_ids=true | all-gather | bytes 331776 | tf_op jit(solution)/shard_map/all_gather | solution.py:113
  96.4 5.2 reshape.263
  108.9 40.5 %while.40 = (s32[]{:T(128)}, bf16[3,512,3,64]{1,3,2,0:T(8,128)(2,1)}, bf16[3,3,512,512]{3,2,1,0:T(8,128)(2,1)}, f32[3,3,512]{2,1,0:T(4,128)}, bf16[3,512,3,64]{1...) while((s32[]{:T(128)}, ...), condition=%wide.region_3.4_spmd, body=%wide.region_0.3_spmd.sunk | while | flops 211909120 | bytes 20769400 | solution.py:136
  157.6 52.0 %all-reduce.7.cloned.1.call-done = bf16[1536,768]{1,0:T(8,128)(2,1)} async-done(((bf16[1536,768]{1,0:T(8,128)(2,1)}), bf16[1536,768]{1,0:T(8,128)(2,1)}) %all-reduce.7.cloned.1.call-update) | async-done | bytes 2359312 | tf_op jit(solution)/shard_map/psum | solution.py:34
  216.3 24.9 %all-gather.9.cloned.1.call-done = bf16[768,768]{0,1:T(8,128)(2,1)} async-done(((bf16[768,96]{0,1:T(8,128)(2,1)}), bf16[768,768]{0,1:T(8,128)(2,1)}) %all-gather.9.cloned.1.call-update) | async-done | bytes 1179664 | tf_op jit(solution)/shard_map/all_gather | solution.py:114
  241.2 16.5 %convolution_convert_fusion.2 = bf16[1536,768]{1,0:T(8,128)(2,1)} fusion(bf16[768,768]{0,1:T(8,128)(2,1)} %all-gather.9.cloned.1.call-done, bf16[1536,768]{1,0:T(8,128)(2,1)} %fusion.110, bf16[768,768]{1,0:T(8,128)(2,1)} %all-gather.7.cloned.1.call-done, f32[768]{0:T(1024)S(1)} %copy-done.36), kind=kOutput, calls=%fused_computation.153 | convolution fusion | flops 3702915072 | bytes 7080960 | tf_op jit(solution)/shard_map/dot_general | solution.py:150
  258.3 6.8 all-gather.11.cloned.1.call-done
  268.3 4.5 copy.120
  272.8 39.2 %all-reduce.9.cloned.1.call-done = bf16[1536,768]{1,0:T(8,128)(2,1)} async-done(((bf16[1536,768]{1,0:T(8,128)(2,1)}), bf16[1536,768]{1,0:T(8,128)(2,1)}) %all-reduce.9.cloned.1.call-update) | async-done | bytes 2359312 | tf_op jit(solution)/shard_map/psum | solution.py:34
  312.1 4.6 fusion.125
  319.4 4.4 fusion.97
  330.4 14.0 %fusion.159 = (f32[768]{0:T(1024)S(1)}, bf16[1536,768]{1,0:T(8,128)(2,1)S(1)}, f32[1536,768]{1,0:T(8,128)}) fusion(f32[1536,768]{1,0:T(8,128)S(1)} %fusion.171, f32[768]{0:T(1024)S(1)} %copy-done.36, bf16[1536,768]{1,0:T(8,128)(2,1)S(1)} %get-tuple-element.432, bf16[768,768]{0,1:T(8,128)(2,1)S(1)} %copy-done.35), kind=kOutput, calls=%fused_computation.235 | convolution fusion | flops 1899232512 | bytes 15341568 | tf_op jit(solution)/shard_map/dot_general | solution.py:171
  352.9 6.7 reshape.265
  366.3 38.8 %all-reduce.11.cloned.1.call-done = bf16[1536,768]{1,0:T(8,128)(2,1)} async-done(((bf16[1536,768]{1,0:T(8,128)(2,1)}), bf16[1536,768]{1,0:T(8,128)(2,1)}) %all-reduce.11.cloned.1.call-update) | async-done | bytes 2359312 | tf_op jit(solution)/shard_map/psum | solution.py:34
  405.1 5.8 multiply_reduce_fusion.1
  411.1 4.6 fusion.158
  422.8 46.1 %while.41 = (s32[]{:T(128)}, f32[3,512,3,64]{1,3,2,0:T(8,128)}, bf16[3,512,3,64]{1,3,2,0:T(8,128)(2,1)}, f32[3,512,3,64]{1,3,2,0:T(8,128)}, bf16[3,3,512,512]{3,...) while((s32[]{:T(128)}, f32[3,512,3,64]{1,3,2,0:T(8,128)}, ...), condition=%wide.region_17.18_spmd, body=%wide.region_15.17_spmd.sunk | while | flops 512424448 | bytes 34580112 | solution.py:203
  479.8 23.6 %while.42 = (s32[]{:T(128)}, bf16[3,512,3,64]{1,3,2,0:T(8,128)(2,1)S(1)}, bf16[3,512,3,64]{1,3,2,0:T(8,128)(2,1)}, s32[3,512]{1,0:T(4,128)}, bf16[3,512,3,64]{1,...) while((s32[]{:T(128)}, ...), condition=%wide.region_26.27_spmd, body=%wide.region_23.26_spmd.sunk | while | flops 312576512 | bytes 5136481 | solution.py:136
  504.1 5.3 fusion.121
  509.4 7.4 fusion.113
  527.0 39.7 %all-reduce = (f32[2,192]{1,0:T(2,128)}, f32[768]{0:T(1024)}, f32[1,768]{1,0:T(1,128)S(1)}, f32[1,768]{1,0:T(1,128)S(1)}, f32[1,768]{1,0:T(1,128)S(1)}, /*index=...) all-reduce(f32[2,192]{1,0:T(2,128)S(1)} %pad_maximum_fusion.5, ...), channel_id=1, replica_groups=mesh['dp'=8,'tensor'=4] {'dp'}, use_global_device_ids=true, to_apply=%region_22.23 | all-reduce | flops 5760 | bytes 46080 | tf_op jit(solution)/shard_map/psum | solution.py:233
  573.2 184.3 %all-reduce.13.cloned.1.call-done = (f32[768,3,192]{0,2,1:T(8,128)}, f32[192,768]{1,0:T(8,128)}, f32[768,768]{1,0:T(8,128)}, f32[768,768]{1,0:T(8,128)}) async-done(((f32[768,3,192]{0,2,1:T(8,128)}, f32[192,768]{1,0:T(8,128)}, f32[768,768]{1,0:T(8,128)}, f32[768,768]{1,0:T(8,128)}), (f32[768,3,192]{0,2,1:T(8,128)}, f32[192,768]{1,0:T(8,128)}, f32[768,768]{1,0:T(8,128)}, ...) | async-done | bytes 7077904 | tf_op jit(solution)/shard_map/psum | solution.py:233
  (259 shorter events, 212.3 us)
Async XLA Ops:
  8.0 82.7 %all-gather.5.cloned.1.call-start = ((), (), s32[]{:S(2)}) async-start(), calls=%async_computation.1 | async-start | bytes 2949120 | tf_op jit(solution)/shard_map/all_gather | solution.py:103
  8.7 200.9 %all-reduce.7.cloned.1.call-start = ((), (), s32[]{:S(2)}) async-start(), calls=%async_computation.2 | async-start | bytes 4718592 | tf_op jit(solution)/shard_map/psum | solution.py:34
  50.6 43.0 %copy-start.20 = (bf16[768,3,192]{0,2,1:T(8,128)(2,1)}, bf16[768,3,192]{0,2,1:T(8,128)(2,1)S(1)}, u32[]{:S(2)}) copy-start(bf16[768,3,192]{0,2,1:T(8,128)(2,1)S(1)} %copy.113) | copy-start | bytes 2654212
  50.6 40.0 %copy-start.33 = (f32[2,192]{1,0:T(2,128)S(1)}, f32[2,192]{1,0:T(2,128)}, u32[]{:S(2)}) copy-start(f32[2,192]{1,0:T(2,128)} %param.24) | copy-start | bytes 4612
  93.6 317.4 %copy-start = (bf16[3,512,768]{2,1,0:T(8,128)(2,1)}, bf16[3,512,768]{2,1,0:T(8,128)(2,1)S(1)}, u32[]{:S(2)}) copy-start(bf16[3,512,768]{2,1,0:T(8,128)(2,1)S(1)} %copy.111) | copy-start | bytes 7077892
  149.4 5.9 copy-start.24
  151.1 5.9 copy-start.32
  154.6 61.8 %all-gather.7.cloned.1.call-start = ((), (), s32[]{:S(2)}) async-start(), calls=%async_computation.3 | async-start | bytes 1327104 | tf_op jit(solution)/shard_map/all_gather | solution.py:110
  155.3 85.9 %all-gather.9.cloned.1.call-start = ((), (), s32[]{:S(2)}) async-start(), calls=%async_computation.4 | async-start | bytes 1327104 | tf_op jit(solution)/shard_map/all_gather | solution.py:114
  156.1 109.0 %all-gather.11.cloned.1.call-start = ((), (), s32[]{:S(2)}) async-start(), calls=%async_computation.6 | async-start | bytes 2949120 | tf_op jit(solution)/shard_map/all_gather | solution.py:104
  156.7 155.4 %all-reduce.9.cloned.1.call-start = ((), (), s32[]{:S(2)}) async-start(), calls=%async_computation.5 | async-start | bytes 4718592 | tf_op jit(solution)/shard_map/psum | solution.py:34
  157.0 166.8 %copy-start.25 = (f32[768]{0:T(1024)}, f32[768]{0:T(1024)S(1)}, u32[]{:S(2)}) copy-start(f32[768]{0:T(1024)S(1)} %get-tuple-element.353) | copy-start | bytes 9220
  213.6 27.6 %copy-start.36 = (f32[768]{0:T(1024)S(1)}, f32[768]{0:T(1024)}, u32[]{:S(2)}) copy-start(f32[768]{0:T(1024)} %param.27) | copy-start | bytes 9220
  257.8 147.4 %all-reduce.11.cloned.1.call-start = ((), (), s32[]{:S(2)}) async-start(), calls=%async_computation.7 | async-start | bytes 4718592 | tf_op jit(solution)/shard_map/psum | solution.py:34
  330.4 14.0 %copy-start.37 = (f32[1536,768]{1,0:T(8,128)}, f32[1536,768]{1,0:T(8,128)S(1)}, u32[]{:S(2)}) copy-start(f32[1536,768]{1,0:T(8,128)S(1)} %fusion.171) | copy-start | bytes 14155780
  349.2 219.3 %reduce-scatter.4.cloned.1.call-start = ((), (), s32[]{:S(2)}) async-start(), calls=%async_computation.8 | async-start | bytes 2949120
  405.1 5.9 copy-start.11
  411.1 6.8 copy-start.12
  479.6 277.8 %all-reduce.13.cloned.1.call-start = ((), (), s32[]{:S(2)}) async-start(), calls=%async_computation.9 | async-start | bytes 14155776 | tf_op jit(solution)/shard_map/psum | solution.py:233
  479.8 24.3 %copy-start.10 = (bf16[1536,768]{1,0:T(8,128)(2,1)S(1)}, bf16[1536,768]{1,0:T(8,128)(2,1)}, u32[]{:S(2)}) copy-start(bf16[1536,768]{1,0:T(8,128)(2,1)} %fusion.110) | copy-start | bytes 7077892
  503.4 6.0 copy-start.14
  504.1 12.7 %slice-start = ((s8[4718592]{0:T(1024)(128)(4,1)}), s8[4194304]{0:T(1024)(128)(4,1)S(1)}, s32[]{:S(2)}) async-start(s8[4718592]{0:T(1024)(128)(4,1)} %bitcast.304), calls=%async_computation.10 | async-start | bytes 8388608
  509.4 7.4 slice-start.1
  757.5 6.3 copy-start.16
  (25 other events, 88.2 us)
Sparse Core Ops, SparseCore 0:
  10.4 26.7 all-gather.4
  154.7 54.9 all-reduce.6
  257.9 54.1 all-reduce.8
  349.4 55.7 all-reduce.10
  479.8 33.1 reduce-scatter.3
Sparse Core Ops, SparseCore 1:
  157.8 40.7 all-gather.6
  201.2 40.0 all-gather.8
  242.6 22.4 all-gather.10
  522.1 235.4 all-reduce.12
where the time goes:
time: 782 us; the launch traced here: 773 us
  waiting for transfers between devices  347 us (44%)
  matrix products  135 us (17%)
  blocking collectives  112 us (14%)
  local copies, waits for them, and re-layouts  99 us (13%)
  other arithmetic  61.8 us (8%)
  between operations  16.5 us (2%)
    psum x1, waiting for transfers between devices, body(): lax.psum((grad_qkv, grad_b_qv, grad_out, grad_bias_out, grad_gain_one, gr...  184 us
    psum x3, waiting for transfers between devices, branch_total(): lax.psum(partial_value.astype(jnp.bfloat16), 'tensor').astype(jnp.float32)  130 us
    psum x1, blocking collectives, body(): lax.psum((grad_qkv, grad_b_qv, grad_out, grad_bias_out, grad_gain_one, gr...  39.7 us
    all_gather x1, blocking collectives, body(): lax.all_gather(w_qkv.astype(jnp.bfloat16), 'dp', axis=0, tiled=True)  38.8 us
    all_gather x1, blocking collectives, body(): lax.all_gather(w_out.astype(jnp.bfloat16), 'dp', axis=1, tiled=True)  33 us
    all_gather x1, waiting for transfers between devices, body(): lax.all_gather(w_down.astype(jnp.bfloat16), 'dp', axis=1, tiled=True)  24.9 us
    dynamic_update_slice x12, local copies, waits for them, and re-layouts, attend_all(): lax.map(one_row, (packed[:, :, 0], packed[:, :, 1], packed[:, :, 2], prev...  21.5 us
    unnamed x91, local copies, waits for them, and re-layouts  20.5 us
  transfers between devices with their start and end apart: 9, of which 6 were waited for; matrix products, arithmetic and copies ran while one was open for 15% of the time, Pallas kernels for 0%

commit v1 on v0

--- a/solution.py
+++ b/solution.py
@@ -6,6 +6,10 @@
 
 EPS = 1e-06
 NEG = -1e30
+
+
+def group_measure(incoming_x):
+    return jnp.sum(lax.all_gather(incoming_x, "tensor"), 0)
 
 
 def gelu_exact(values):
@@ -31,7 +35,7 @@
 
 
 def branch_total(partial_value):
-    return lax.psum(partial_value.astype(jnp.bfloat16), "tensor").astype(jnp.float32)
+    return group_measure(partial_value.astype(jnp.bfloat16)).astype(jnp.float32)
 
 
 def attend_rows(query, keys, values, previous, segment, inv_root):

time: 782 us -> 896 us (1.15)
  waiting for transfers between devices: 347 us -> 429 us
  other arithmetic: 61.8 us -> 104 us
  local copies, waits for them, and re-layouts: 99 us -> 89.1 us
    all_gather x0 -> x3, waiting for transfers between devices: none -> 168 us  [group_measure(): return jnp.sum(lax.all_gather(incoming_x, 'tensor'), 0)]
    psum x3 -> x0, waiting for transfers between devices: 130 us -> none  [branch_total(): lax.psum(partial_value.astype(jnp.bfloat16), 'tensor').astype(jnp.float32)]
    all_gather x1, waiting for transfers between devices: 0.01 us -> 42.5 us  [body(): lax.all_gather(w_up.astype(jnp.bfloat16), 'dp', axis=0, tiled=True)]
    reduce_sum x2 -> x4, other arithmetic: 7.79 us -> 26.3 us  [the longest x3 21.5 us: group_measure(): return jnp.sum(lax.all_gather(incoming_x, 'tensor'), 0)]
    convert_element_type x1, other arithmetic: 2.86 us -> 14.8 us  [body(): grad_sum_two_bf = grad_sum_two.astype(jnp.bfloat16)]
    dynamic_update_slice x12, local copies, waits for them, and re-layouts: 21.5 us -> 11.7 us  [attend_all(): lax.map(one_row, (packed[:, :, 0], packed[:, :, 1], packed[:, :, 2], prev...]
    unnamed x91 -> x139, local copies, waits for them, and re-layouts: 20.5 us -> 17.9 us
  transfers between devices with their start and end apart: 9 -> 9, of which waited for: 6 -> 7; matrix products, arithmetic and copies ran while one was open for 15% -> 14% of each run, Pallas kernels for 0% -> 0%
where the time goes in v1:
time: 896 us; the launch traced here: 887 us
  waiting for transfers between devices  429 us (48%)
  matrix products  138 us (15%)
  blocking collectives  110 us (12%)
  other arithmetic  104 us (12%)
  local copies, waits for them, and re-layouts  89.1 us (10%)
  between operations  15.2 us (2%)
    psum x1, waiting for transfers between devices, body(): lax.psum((grad_qkv, grad_b_qv, grad_out, grad_bias_out, grad_gain_one, gr...  185 us
    all_gather x3, waiting for transfers between devices, group_measure(): return jnp.sum(lax.all_gather(incoming_x, 'tensor'), 0)  168 us
    all_gather x1, waiting for transfers between devices, body(): lax.all_gather(w_up.astype(jnp.bfloat16), 'dp', axis=0, tiled=True)  42.5 us
    psum x1, blocking collectives, body(): lax.psum((grad_qkv, grad_b_qv, grad_out, grad_bias_out, grad_gain_one, gr...  40.1 us
    all_gather x1, blocking collectives, body(): lax.all_gather(w_qkv.astype(jnp.bfloat16), 'dp', axis=0, tiled=True)  38.8 us
    all_gather x1, blocking collectives, body(): lax.all_gather(w_out.astype(jnp.bfloat16), 'dp', axis=1, tiled=True)  31.2 us
    all_gather x1, waiting for transfers between devices, body(): lax.all_gather(w_down.astype(jnp.bfloat16), 'dp', axis=1, tiled=True)  25.1 us
    reduce_sum x3, other arithmetic, group_measure(): return jnp.sum(lax.all_gather(incoming_x, 'tensor'), 0)  21.5 us
  transfers between devices with their start and end apart: 9, of which 7 were waited for; matrix products, arithmetic and copies ran while one was open for 14% of the time, Pallas kernels for 0%

profile of v1, /device:TPU:0, one launch (start us, length us, event | category | flops | bytes accessed | tf_op | source)
XLA Modules:
  0.0 887.0 jit_solution(12806196466580323640)
XLA Ops:
  9.1 38.8 %all_gather.37 = bf16[768,3,192]{2,1,0:T(4,128)(2,1)S(1)} all-gather(bf16[96,3,192]{2,1,0:T(4,128)(2,1)S(1)} %copy.116), channel_id=1, replica_groups=mesh['dp'=8,'tensor'=4] {'dp'}, dimensions={0}, use_global_device_ids=true | all-gather | bytes 995328 | tf_op jit(solution)/shard_map/all_gather | solution.py:113
  50.0 6.7 copy.121
  56.8 31.2 %all_gather.38 = bf16[192,768]{0,1:T(8,128)(2,1)S(1)} all-gather(bf16[192,96]{0,1:T(8,128)(2,1)S(1)} %copy.123), channel_id=1, replica_groups=mesh['dp'=8,'tensor'=4] {'dp'}, dimensions={1}, use_global_device_ids=true | all-gather | bytes 331776 | tf_op jit(solution)/shard_map/all_gather | solution.py:117
  109.7 28.1 %while.40 = (s32[]{:T(128)}, bf16[3,512,3,64]{1,3,2,0:T(8,128)(2,1)}, bf16[3,3,512,512]{3,2,1,0:T(8,128)(2,1)}, f32[3,3,512]{2,1,0:T(4,128)}, bf16[3,512,3,64]{1...) while((s32[]{:T(128)}, ...), condition=%wide.region_3.4_spmd, body=%wide.region_0.3_spmd.sunk | while | flops 211909120 | bytes 20769400 | solution.py:140
  144.9 60.2 %all-gather.19.cloned.1.call-done = bf16[6144,768]{1,0:T(8,128)(2,1)} async-done(((bf16[1536,768]{1,0:T(8,128)(2,1)}), bf16[6144,768]{1,0:T(8,128)(2,1)}) %all-gather.19.cloned.1.call-update) | async-done | bytes 9437200 | tf_op jit(solution)/shard_map/all_gather | solution.py:12
  205.1 7.3 reduce_sum.216
  223.9 25.1 %all-gather.15.cloned.1.call-done = bf16[768,768]{0,1:T(8,128)(2,1)} async-done(((bf16[768,96]{0,1:T(8,128)(2,1)}), bf16[768,768]{0,1:T(8,128)(2,1)}) %all-gather.15.cloned.1.call-update) | async-done | bytes 1179664 | tf_op jit(solution)/shard_map/all_gather | solution.py:118
  249.0 42.5 %all-gather.13.cloned.1.call-done = bf16[768,768]{1,0:T(8,128)(2,1)} async-done(((bf16[96,768]{1,0:T(8,128)(2,1)}), bf16[768,768]{1,0:T(8,128)(2,1)}) %all-gather.13.cloned.1.call-update) | async-done | bytes 1179664 | tf_op jit(solution)/shard_map/all_gather | solution.py:114
  291.4 16.5 %convolution_convert_fusion.2 = bf16[1536,768]{1,0:T(8,128)(2,1)} fusion(bf16[768,768]{0,1:T(8,128)(2,1)} %all-gather.15.cloned.1.call-done, bf16[1536,768]{1,0:T(8,128)(2,1)} %fusion.112, bf16[768,768]{1,0:T(8,128)(2,1)} %all-gather.13.cloned.1.call-done, f32[768]{0:T(1024)S(1)} %copy-done.57), kind=kOutput, calls=%fused_computation.157 | convolution fusion | flops 3702915072 | bytes 7080960 | tf_op jit(solution)/shard_map/dot_general | solution.py:154
  308.4 7.3 all-gather.17.cloned.1.call-done
  320.0 62.0 %all-gather.21.cloned.1.call-done = bf16[6144,768]{1,0:T(8,128)(2,1)} async-done(((bf16[1536,768]{1,0:T(8,128)(2,1)}), bf16[6144,768]{1,0:T(8,128)(2,1)}) %all-gather.21.cloned.1.call-update) | async-done | bytes 9437200 | tf_op jit(solution)/shard_map/all_gather | solution.py:12
  382.0 7.1 reduce_sum.219
  402.9 14.8 %fusion.159 = (bf16[1536,768]{1,0:T(8,128)(2,1)S(1)}, f32[1536,768]{1,0:T(8,128)}) fusion(f32[1536]{0:T(1024)S(1)} %rsqrt.27, f32[1536]{0:T(1024)S(1)} %div.61, f32[1536]{0:T(1024)S(1)} %div.59, f32[768]{0:T(1024)S(1)} %get-tuple-element.354, bf16[3,512,768]{2,1,0:T(8,128)(2,1)} %copy.125, f32[1536]{0:T(1024)S(1)} %div.56, f32[768]{0:T(1024)S(1)} %get-tuple-element.358, ...), kind=kLoop, calls=%fused_computation.237 | loop fusion | flops 23592960 | bytes 16567296 | tf_op jit(solution)/shard_map/convert_element_type | solution.py:167
  419.9 14.7 %fusion.160 = (f32[768]{0:T(1024)}, bf16[1536,768]{1,0:T(8,128)(2,1)S(1)}, f32[1536,768]{1,0:T(8,128)}) fusion(f32[1536,768]{1,0:T(8,128)S(1)} %fusion.174, f32[768]{0:T(1024)S(1)} %copy-done.57, bf16[1536,768]{1,0:T(8,128)(2,1)S(1)} %get-tuple-element.432, bf16[768,768]{0,1:T(8,128)(2,1)S(1)} %copy-done.55), kind=kOutput, calls=%fused_computation.238 | convolution fusion | flops 1899232512 | bytes 15341568 | tf_op jit(solution)/shard_map/dot_general | solution.py:175
  444.2 6.9 reshape.985
  458.3 45.6 %all-gather.23.cloned.1.call-done = bf16[6144,768]{1,0:T(8,128)(2,1)} async-done(((bf16[1536,768]{1,0:T(8,128)(2,1)}), bf16[6144,768]{1,0:T(8,128)(2,1)}) %all-gather.23.cloned.1.call-update) | async-done | bytes 9437200 | tf_op jit(solution)/shard_map/all_gather | solution.py:12
  504.0 7.1 reduce_sum.224
  511.2 10.1 %multiply_reduce_fusion.1 = (f32[768]{0:T(1024)}, f32[768]{0:T(1024)}, f32[3,512]{1,0:T(4,128)S(1)}, f32[3,512]{1,0:T(4,128)S(1)}, f32[3,512,768]{2,1,0:T(8,128)}) fusion(bf16[3,512,768]{2,1,0:T(8,128)(2,1)} %copy.125, f32[3,512,768]{2,1,0:T(8,128)} %get-tuple-element.435, f32[3,512]{1,0:T(4,128)S(1)} %copy-done.27, ...), kind=kLoop, calls=%fused_computation.103 | loop fusion | flops 22408704 | bytes 18935808 | tf_op jit(solution)/shard_map/reduce_sum | solution.py:163
  521.4 6.4 subtract_multiply_fusion.1
  535.0 46.3 %while.41 = (s32[]{:T(128)}, f32[3,512,3,64]{1,3,2,0:T(8,128)}, bf16[3,512,3,64]{1,3,2,0:T(8,128)(2,1)}, f32[3,512,3,64]{1,3,2,0:T(8,128)}, bf16[3,3,512,512]{3,...) while((s32[]{:T(128)}, f32[3,512,3,64]{1,3,2,0:T(8,128)}, ...), condition=%wide.region_17.18_spmd, body=%wide.region_15.17_spmd.sunk | while | flops 512424448 | bytes 34580112 | solution.py:207
  592.2 23.6 %while.42 = (s32[]{:T(128)}, bf16[3,512,3,64]{1,3,2,0:T(8,128)(2,1)S(1)}, bf16[3,512,3,64]{1,3,2,0:T(8,128)(2,1)}, s32[3,512]{1,0:T(4,128)}, bf16[3,512,3,64]{1,...) while((s32[]{:T(128)}, ...), condition=%wide.region_26.27_spmd, body=%wide.region_23.26_spmd.sunk | while | flops 312576512 | bytes 5136481 | solution.py:140
  621.9 7.4 fusion.114
  640.7 40.1 %all-reduce = (f32[2,192]{1,0:T(2,128)}, f32[768]{0:T(1024)}, f32[1,768]{1,0:T(1,128)S(1)}, f32[1,768]{1,0:T(1,128)S(1)}, f32[1,768]{1,0:T(1,128)S(1)}, /*index=...) all-reduce(f32[2,192]{1,0:T(2,128)S(1)} %pad_maximum_fusion.5, ...), channel_id=1, replica_groups=mesh['dp'=8,'tensor'=4] {'dp'}, use_global_device_ids=true, to_apply=%region_22.23 | all-reduce | flops 5760 | bytes 46080 | tf_op jit(solution)/shard_map/psum | solution.py:237
  687.4 185.0 %all-reduce.4.cloned.1.call-done = (f32[768,3,192]{0,2,1:T(8,128)}, f32[192,768]{1,0:T(8,128)}, f32[768,768]{1,0:T(8,128)}, f32[768,768]{1,0:T(8,128)}) async-done(((f32[768,3,192]{0,2,1:T(8,128)}, f32[192,768]{1,0:T(8,128)}, f32[768,768]{1,0:T(8,128)}, f32[768,768]{1,0:T(8,128)}), (f32[768,3,192]{0,2,1:T(8,128)}, f32[192,768]{1,0:T(8,128)}, f32[768,768]{1,0:T(8,128)}, ...) | async-done | bytes 7077904 | tf_op jit(solution)/shard_map/psum | solution.py:237
  (318 shorter events, 228.2 us)
Async XLA Ops:
  7.2 80.9 %all-gather.11.cloned.1.call-start = ((), (), s32[]{:S(2)}) async-start(), calls=%async_computation.1 | async-start | bytes 2949120 | tf_op jit(solution)/shard_map/all_gather | solution.py:107
  7.9 197.2 %all-gather.19.cloned.1.call-start = ((), (), s32[]{:S(2)}) async-start(), calls=%async_computation.5 | async-start | bytes 11796480 | tf_op jit(solution)/shard_map/all_gather | solution.py:12
  50.0 38.0 %copy-start.54 = (f32[2,192]{1,0:T(2,128)S(1)}, f32[2,192]{1,0:T(2,128)}, u32[]{:S(2)}) copy-start(f32[2,192]{1,0:T(2,128)} %param.24) | copy-start | bytes 4612
  141.8 107.1 %all-gather.15.cloned.1.call-start = ((), (), s32[]{:S(2)}) async-start(), calls=%async_computation.3 | async-start | bytes 1327104 | tf_op jit(solution)/shard_map/all_gather | solution.py:118
  142.6 148.8 %all-gather.13.cloned.1.call-start = ((), (), s32[]{:S(2)}) async-start(), calls=%async_computation.2 | async-start | bytes 1327104 | tf_op jit(solution)/shard_map/all_gather | solution.py:114
  143.3 172.4 %all-gather.17.cloned.1.call-start = ((), (), s32[]{:S(2)}) async-start(), calls=%async_computation.4 | async-start | bytes 2949120 | tf_op jit(solution)/shard_map/all_gather | solution.py:108
  143.9 238.0 %all-gather.21.cloned.1.call-start = ((), (), s32[]{:S(2)}) async-start(), calls=%async_computation.6 | async-start | bytes 11796480 | tf_op jit(solution)/shard_map/all_gather | solution.py:12
  144.2 258.6 %copy-start.30 = (f32[768]{0:T(1024)}, f32[768]{0:T(1024)S(1)}, u32[]{:S(2)}) copy-start(f32[768]{0:T(1024)S(1)} %get-tuple-element.359) | copy-start | bytes 9220
  144.9 257.9 %copy-start.19 = (f32[768]{0:T(1024)}, f32[768]{0:T(1024)S(1)}, u32[]{:S(2)}) copy-start(f32[768]{0:T(1024)S(1)} %get-tuple-element.355) | copy-start | bytes 9220
  144.9 257.9 %copy-start.28 = (f32[768]{0:T(1024)}, f32[768]{0:T(1024)S(1)}, u32[]{:S(2)}) copy-start(f32[768]{0:T(1024)S(1)} %get-tuple-element.354) | copy-start | bytes 9220
  217.0 185.9 %copy-start.22 = (f32[1536]{0:T(1024)}, f32[1536]{0:T(1024)S(1)}, u32[]{:S(2)}) copy-start(f32[1536]{0:T(1024)S(1)} %div.53) | copy-start | bytes 18436
  219.9 71.5 %copy-start.57 = (f32[768]{0:T(1024)S(1)}, f32[768]{0:T(1024)}, u32[]{:S(2)}) copy-start(f32[768]{0:T(1024)} %param.27) | copy-start | bytes 9220
  219.9 169.1 %copy-start.16 = (f32[3,512]{1,0:T(4,128)}, f32[3,512]{1,0:T(4,128)S(1)}, u32[]{:S(2)}) copy-start(f32[3,512]{1,0:T(4,128)S(1)} %add_rsqrt_fusion.1) | copy-start | bytes 18436
  220.0 182.9 %copy-start.24 = (f32[1536]{0:T(1024)}, f32[1536]{0:T(1024)S(1)}, u32[]{:S(2)}) copy-start(f32[1536]{0:T(1024)S(1)} %rsqrt.25) | copy-start | bytes 18436
  308.0 195.9 %all-gather.23.cloned.1.call-start = ((), (), s32[]{:S(2)}) async-start(), calls=%async_computation.7 | async-start | bytes 11796480 | tf_op jit(solution)/shard_map/all_gather | solution.py:12
  397.4 20.4 %copy-start.26 = (f32[3,512]{1,0:T(4,128)}, f32[3,512]{1,0:T(4,128)S(1)}, u32[]{:S(2)}) copy-start(f32[3,512]{1,0:T(4,128)S(1)} %add_rsqrt_fusion) | copy-start | bytes 18436
  397.4 20.4 %copy-start.33 = (f32[1536]{0:T(1024)}, f32[1536]{0:T(1024)S(1)}, u32[]{:S(2)}) copy-start(f32[1536]{0:T(1024)S(1)} %rsqrt.27) | copy-start | bytes 18436
  402.2 15.5 %copy-start.35 = (f32[1536]{0:T(1024)}, f32[1536]{0:T(1024)S(1)}, u32[]{:S(2)}) copy-start(f32[1536]{0:T(1024)S(1)} %div.61) | copy-start | bytes 18436
  402.8 15.0 %copy-start.41 = (f32[3,512]{1,0:T(4,128)}, f32[3,512]{1,0:T(4,128)S(1)}, u32[]{:S(2)}) copy-start(f32[3,512]{1,0:T(4,128)S(1)} %broadcast_multiply_fusion.3) | copy-start | bytes 18436
  402.9 14.9 %copy-start.4 = (bf16[1536,768]{1,0:T(8,128)(2,1)S(1)}, bf16[1536,768]{1,0:T(8,128)(2,1)}, u32[]{:S(2)}) copy-start(bf16[1536,768]{1,0:T(8,128)(2,1)} %fusion.112) | copy-start | bytes 7077892
  402.9 14.9 %copy-start.56 = (bf16[768,768]{1,0:T(8,128)(2,1)S(1)}, bf16[768,768]{1,0:T(8,128)(2,1)}, u32[]{:S(2)}) copy-start(bf16[768,768]{1,0:T(8,128)(2,1)} %all-gather.13.cloned.1.call-done) | copy-start | bytes 3538948
  439.5 243.1 %reduce-scatter.4.cloned.1.call-start = ((), (), s32[]{:S(2)}) async-start(), calls=%async_computation.8 | async-start | bytes 2949120
  592.1 280.3 %all-reduce.4.cloned.1.call-start = ((), (), s32[]{:S(2)}) async-start(), calls=%async_computation.9 | async-start | bytes 14155776 | tf_op jit(solution)/shard_map/psum | solution.py:237
  592.2 24.3 %copy-start.5 = (bf16[1536,768]{1,0:T(8,128)(2,1)S(1)}, bf16[1536,768]{1,0:T(8,128)(2,1)}, u32[]{:S(2)}) copy-start(bf16[1536,768]{1,0:T(8,128)(2,1)} %fusion.112) | copy-start | bytes 7077892
  (49 other events, 320.1 us)
Sparse Core Ops, SparseCore 0:
  9.6 26.7 all-gather.10
  141.9 63.1 all-gather.18
  207.9 41.0 all-gather.14
  251.6 39.8 all-gather.12
  292.8 22.8 all-gather.16
  317.7 64.2 all-gather.20
  439.7 64.2 all-gather.22
  592.2 33.0 reduce-scatter.3
  635.8 236.5 all-reduce.3
